TPU v7x, 256 devices: a whole 4x4x8 slice. The times are simulated.
256 devices in a mesh: row: 32 (over z, y_lo, core), col: 8 (over x, y_hi).
Axes of the slice: x: 4, y: 4 (y_hi: 2, y_lo: 2; y = y_hi * 2 + y_lo), z: 8, core: 2. Of those that a mesh axis runs over, the one named last changes fastest.
Arguments:
- activations: bfloat16 [1024, 16384], P('col', 'row'), may hold values from -6 to 6
- out_grad: bfloat16 [1024, 16384], P('col', 'row'), may hold values from -2 to 2
- gate_pre: bfloat16 [1024, 8192], P('row', 'col'), may hold values from -6 to 6
- up_pre: bfloat16 [1024, 8192], P('row', 'col'), may hold values from -6 to 6
- gate_weight: bfloat16 [16384, 8192], P('row', 'col'), may hold values from -0.046875 to 0.046875
- up_weight: bfloat16 [16384, 8192], P('row', 'col'), may hold values from -0.046875 to 0.046875
- down_weight: bfloat16 [8192, 16384], P('col', 'row'), may hold values from -0.0625 to 0.0625
Outputs:
- input_grad: bfloat16 [1024, 16384], P('col', 'row')
- gate_grad: bfloat16 [16384, 8192], P('row', 'col')
- up_grad: bfloat16 [16384, 8192], P('row', 'col')
- down_grad: bfloat16 [8192, 16384], P('col', 'row')
All inputs are finite; a program needn't handle non-finite values.
Results may differ from a plain program's by a relative error of at most 0.0051.
Values may be sent and summed in bfloat16 or wider, within the bound.
A program may use at most 64 MiB of HBM per device.

v0:
```python
import jax
import jax.numpy as jnp
from jax import lax
from jax.sharding import PartitionSpec as P


def contract_rows(left, right):
    return lax.dot_general(
        left, right, (((0,), (0,)), ((), ())), preferred_element_type=jnp.float32
    )


def contract_cols(left, right):
    return lax.dot_general(
        left, right, (((1,), (1,)), ((), ())), preferred_element_type=jnp.float32
    )


def derive(hidden_grad, gate_pre, up_pre):
    gate_val = gate_pre.astype(jnp.float32)
    up_val = up_pre.astype(jnp.float32)
    gate_sig = jax.nn.sigmoid(gate_val)
    swish_val = gate_val * gate_sig
    hidden = (swish_val * up_val).astype(jnp.bfloat16)
    gate_back = (hidden_grad * up_val * gate_sig * (1.0 + gate_val * (1.0 - gate_sig))).astype(
        jnp.bfloat16
    )
    up_back = (hidden_grad * swish_val).astype(jnp.bfloat16)
    return (hidden, gate_back, up_back)


def per_device(activations, out_grad, gate_pre, up_pre, gate_weight, up_weight, down_weight):
    acts_all, grad_all = (
        lax.all_gather(activations, "col", axis=0, tiled=True),
        lax.all_gather(out_grad, "col", axis=0, tiled=True),
    )
    grad_rows = grad_all
    hidden_grad = lax.psum_scatter(
        contract_cols(grad_rows, down_weight), "row", scatter_dimension=0, tiled=True
    )
    hidden, gate_back, up_back = derive(hidden_grad, gate_pre, up_pre)
    hid_piece = lax.all_gather(hidden, "row", axis=0, tiled=True)
    gate_piece = lax.all_gather(gate_back, "row", axis=0, tiled=True)
    up_piece = lax.all_gather(up_back, "row", axis=0, tiled=True)
    grad_rows = grad_all
    down_acc = contract_rows(hid_piece, grad_rows)
    gate_acc = contract_rows(acts_all, gate_piece)
    up_acc = contract_rows(acts_all, up_piece)
    input_rows = contract_cols(gate_piece, gate_weight) + contract_cols(up_piece, up_weight)
    input_acc = input_rows
    down_acc, gate_acc, up_acc, input_acc = (down_acc, gate_acc, up_acc, input_acc)
    input_grad = lax.psum_scatter(input_acc, "col", scatter_dimension=0, tiled=True)
    return (
        input_grad.astype(jnp.bfloat16),
        gate_acc.astype(jnp.bfloat16),
        up_acc.astype(jnp.bfloat16),
        down_acc.astype(jnp.bfloat16),
    )


def solution(mesh):
    placed = (
        P("col", "row"),
        P("col", "row"),
        P("row", "col"),
        P("row", "col"),
        P("row", "col"),
        P("row", "col"),
        P("col", "row"),
    )
    return jax.shard_map(
        per_device,
        mesh=mesh,
        in_specs=placed,
        out_specs=(P("col", "row"), P("row", "col"), P("row", "col"), P("col", "row")),
        check_vma=False,
    )
```

profile of v0, /device:TPU:1, one launch (start us, length us, event | category | flops | bytes accessed | tf_op | source)
XLA Modules:
  0.0 538.5 jit_solution(6172015009212809988)
XLA Ops:
  7.2 0.0 copy-start
  7.2 0.0 all-gather.6.cloned.1.call-start
  7.2 0.7 all-gather.6.cloned.1.call-update
  7.9 0.0 reduce-scatter.3.cloned.1.call-start
  8.0 57.1 %all-gather.6.cloned.1.call-done = bf16[1024,512]{1,0:T(8,128)(2,1)} async-done(((bf16[128,512]{1,0:T(8,128)(2,1)}), bf16[1024,512]{1,0:T(8,128)(2,1)}) %all-gather.6.cloned.1.call-update) | async-done | bytes 1048592 | tf_op jit(solution)/shard_map/all_gather | solution.py:35
  65.1 0.0 copy-done
  65.1 4.4 fusion.10
  69.5 0.0 copy-start.1
  69.5 0.0 copy-start.2
  69.5 0.0 copy-start.3
  69.5 0.0 reduce-scatter.3.cloned.1.call-update
  69.6 0.0 all-gather.8.cloned.1.call-start
  69.6 122.1 %reduce-scatter.3.cloned.1.call-done = f32[32,1024]{1,0:T(8,128)} async-done(((f32[1024,1024]{1,0:T(8,128)}), f32[32,1024]{1,0:T(8,128)}) %reduce-scatter.3.cloned.1.call-update) | async-done | bytes 131088 | tf_op jit(solution)/shard_map/reduce_scatter | solution.py:38
  191.7 0.0 copy-done.1
  191.7 0.0 copy-done.2
  191.7 1.6 multiply_convert_fusion
  193.4 0.0 all-gather.8.cloned.1.call-update
  193.4 0.0 all-gather.10.cloned.1.call-start
  193.4 0.5 all-gather.10.cloned.1.call-update
  194.0 0.0 all-gather.12.cloned.1.call-start
  194.0 0.5 all-gather.12.cloned.1.call-update
  194.6 0.0 all-gather.14.cloned.1.call-start
  194.6 0.5 all-gather.14.cloned.1.call-update
  195.1 0.0 copy-start.4
  195.1 0.0 reduce-scatter.5.cloned.1.call-start
  195.2 65.6 %all-gather.8.cloned.1.call-done = bf16[1024,1024]{1,0:T(8,128)(2,1)} async-done(((bf16[32,1024]{1,0:T(8,128)(2,1)}), bf16[1024,1024]{1,0:T(8,128)(2,1)}) %all-gather.8.cloned.1.call-update) | async-done | bytes 2097168 | tf_op jit(solution)/shard_map/all_gather | solution.py:43
  260.8 0.0 copy-done.3
  260.8 4.2 fusion.11
  265.0 62.1 %all-gather.10.cloned.1.call-done = bf16[1024,1024]{1,0:T(8,128)(2,1)} async-done(((bf16[32,1024]{1,0:T(8,128)(2,1)}), bf16[1024,1024]{1,0:T(8,128)(2,1)}) %all-gather.10.cloned.1.call-update) | async-done | bytes 2097168 | tf_op jit(solution)/shard_map/all_gather | solution.py:44
  327.1 0.0 copy-done.4
  327.1 4.9 convolution_add_fusion
  332.0 0.0 reduce-scatter.5.cloned.1.call-update
  332.0 47.4 %all-gather.12.cloned.1.call-done = bf16[1024,512]{1,0:T(8,128)(2,1)} async-done(((bf16[128,512]{1,0:T(8,128)(2,1)}), bf16[1024,512]{1,0:T(8,128)(2,1)}) %all-gather.12.cloned.1.call-update) | async-done | bytes 1048592 | tf_op jit(solution)/shard_map/all_gather | solution.py:34
  379.5 3.1 fusion
  382.6 0.0 copy-start.6
  382.6 1.3 copy.11
  383.9 0.0 copy-done.6
  383.9 2.9 fusion.1
  386.8 0.0 copy-start.5
  386.8 1.3 copy.12
  388.1 58.5 %all-gather.14.cloned.1.call-done = bf16[1024,1024]{1,0:T(8,128)(2,1)} async-done(((bf16[32,1024]{1,0:T(8,128)(2,1)}), bf16[1024,1024]{1,0:T(8,128)(2,1)}) %all-gather.14.cloned.1.call-update) | async-done | bytes 2097168 | tf_op jit(solution)/shard_map/all_gather | solution.py:42
  446.6 0.0 copy-done.5
  446.6 3.8 convolution_convert_fusion
  450.5 79.6 %reduce-scatter.5.cloned.1.call-done = f32[128,512]{1,0:T(8,128)} async-done(((f32[1024,512]{1,0:T(8,128)}), f32[128,512]{1,0:T(8,128)}) %reduce-scatter.5.cloned.1.call-update) | async-done | bytes 262160 | tf_op jit(solution)/shard_map/reduce_scatter | solution.py:52
  530.0 1.6 convert_element_type.37
Async XLA Ops:
  7.2 57.9 %copy-start = (bf16[1024,512]{1,0:T(8,128)(2,1)S(1)}, bf16[1024,512]{1,0:T(8,128)(2,1)}, u32[]{:S(2)}) copy-start(bf16[1024,512]{1,0:T(8,128)(2,1)} %param.13) | copy-start | bytes 3145732
  7.2 57.9 %all-gather.6.cloned.1.call-start = ((), (), s32[]{:S(2)}) async-start(), calls=%async_computation.2 | async-start | bytes 1179648 | tf_op jit(solution)/shard_map/all_gather | solution.py:35
  7.9 183.8 %reduce-scatter.3.cloned.1.call-start = ((), (), s32[]{:S(2)}) async-start(), calls=%async_computation.3 | async-start | bytes 4325376 | tf_op jit(solution)/shard_map/reduce_scatter | solution.py:38
  69.5 122.2 %copy-start.1 = (bf16[32,1024]{1,0:T(8,128)(2,1)S(1)}, bf16[32,1024]{1,0:T(8,128)(2,1)}, u32[]{:S(2)}) copy-start(bf16[32,1024]{1,0:T(8,128)(2,1)} %param.9) | copy-start | bytes 196612
  69.5 122.2 %copy-start.2 = (bf16[32,1024]{1,0:T(8,128)(2,1)S(1)}, bf16[32,1024]{1,0:T(8,128)(2,1)}, u32[]{:S(2)}) copy-start(bf16[32,1024]{1,0:T(8,128)(2,1)} %param.10) | copy-start | bytes 196612
  69.5 191.2 %copy-start.3 = (bf16[512,1024]{1,0:T(8,128)(2,1)S(1)}, bf16[512,1024]{1,0:T(8,128)(2,1)}, u32[]{:S(2)}) copy-start(bf16[512,1024]{1,0:T(8,128)(2,1)} %param.11) | copy-start | bytes 3145732
  69.6 191.2 %all-gather.8.cloned.1.call-start = ((), (), s32[]{:S(2)}) async-start(), calls=%async_computation.4 | async-start | bytes 2162688 | tf_op jit(solution)/shard_map/all_gather | solution.py:43
  193.4 133.7 %all-gather.10.cloned.1.call-start = ((), (), s32[]{:S(2)}) async-start(), calls=%async_computation.5 | async-start | bytes 2162688 | tf_op jit(solution)/shard_map/all_gather | solution.py:44
  194.0 185.5 %all-gather.12.cloned.1.call-start = ((), (), s32[]{:S(2)}) async-start(), calls=%async_computation.7 | async-start | bytes 1179648 | tf_op jit(solution)/shard_map/all_gather | solution.py:34
  194.6 252.1 %all-gather.14.cloned.1.call-start = ((), (), s32[]{:S(2)}) async-start(), calls=%async_computation.8 | async-start | bytes 2162688 | tf_op jit(solution)/shard_map/all_gather | solution.py:42
  195.1 132.0 %copy-start.4 = (bf16[512,1024]{1,0:T(8,128)(2,1)S(1)}, bf16[512,1024]{1,0:T(8,128)(2,1)}, u32[]{:S(2)}) copy-start(bf16[512,1024]{1,0:T(8,128)(2,1)} %param.12) | copy-start | bytes 3145732
  195.1 334.9 %reduce-scatter.5.cloned.1.call-start = ((), (), s32[]{:S(2)}) async-start(), calls=%async_computation.6 | async-start | bytes 2359296 | tf_op jit(solution)/shard_map/reduce_scatter | solution.py:52
  382.6 1.3 copy-start.6
  386.8 59.8 %copy-start.5 = (bf16[1024,512]{1,0:T(8,128)(2,1)S(1)}, bf16[1024,512]{1,0:T(8,128)(2,1)}, u32[]{:S(2)}) copy-start(bf16[1024,512]{1,0:T(8,128)(2,1)} %all-gather.6.cloned.1.call-done) | copy-start | bytes 3145732
Sparse Core Ops, SparseCore 0:
  10.6 54.4 all-gather.5
  69.7 121.9 reduce-scatter.2
  194.2 66.5 all-gather.7
  263.1 63.9 all-gather.9
  329.6 49.8 all-gather.11
  381.2 65.3 all-gather.13
  450.7 79.3 reduce-scatter.4
where the time goes:
time: 539 us
  waiting for transfers between devices  495 us (92%)
  matrix products  23.4 us (4%)
  between operations  14.2 us (3%)
    reduce_scatter x1, waiting for transfers between devices, per_device(): lax.psum_scatter(contract_cols(grad_rows, down_weight), 'row', scatter_di...  122 us
    reduce_scatter x1, waiting for transfers between devices, per_device(): lax.psum_scatter(input_acc, 'col', scatter_dimension=0, tiled=True)  79.6 us
    all_gather x1, waiting for transfers between devices, per_device(): gate_piece = lax.all_gather(gate_back, 'row', axis=0, tiled=True)  65.6 us
    all_gather x1, waiting for transfers between devices, per_device(): up_piece = lax.all_gather(up_back, 'row', axis=0, tiled=True)  62.1 us
    all_gather x1, waiting for transfers between devices, per_device(): hid_piece = lax.all_gather(hidden, 'row', axis=0, tiled=True)  58.5 us
    all_gather x1, waiting for transfers between devices, per_device(): lax.all_gather(out_grad, 'col', axis=0, tiled=True)  57.1 us
    all_gather x1, waiting for transfers between devices, per_device(): lax.all_gather(activations, 'col', axis=0, tiled=True)  47.4 us
    dot_general x3, matrix products, contract_cols(): lax.dot_general(left, right, (((1,), (1,)), ((), ())), preferred_element_...  13.6 us
  transfers between devices with their start and end apart: 7, of which 7 were waited for; matrix products, arithmetic and copies ran while one was open for 4% of the time, Pallas kernels for 0%

commit v1 on v0

v1 whole, which is shorter than its diff:
```python
import jax
import jax.numpy as jnp
from jax import lax
from jax.experimental import pallas as pl
from jax.experimental.pallas import tpu as pltpu
from jax.sharding import PartitionSpec as P

MESH = pl.DeviceIdType.MESH
BF = jnp.bfloat16
F32 = jnp.float32
NZ, NX = 8, 4
CH = 2
W = 1024 // CH
N_SEM = 192


def dot_nt(left, right):
    return lax.dot_general(left, right, (((1,), (1,)), ((), ())), preferred_element_type=F32)


def dot_tn(left, right):
    return lax.dot_general(left, right, (((0,), (0,)), ((), ())), preferred_element_type=F32)


def kernel(
    acts, grad, gate, up, gw, uw, dw,
    o_in, o_gate, o_up, o_down,
    acts_all, grad_all, g_all, u_all, hg_all, gw_v, uw_v, dw_v,
    part, rc, qb, zs, zr, zls, zlr, sf, sb, ry,
    a_f, b_f, hid, gb, ub,
    far_s, far_r, near_s, near_r, own_f, ys, yr, in_v, gate_v, up_v, down_v,
    send_sem, recv_sem, loc_sem,
):
    r = lax.axis_index("row")
    c = lax.axis_index("col")
    k = lax.rem(r, 2)
    yl = lax.rem(r // 2, 2)
    z = r // 4
    yh = lax.rem(c, 2)
    x = c // 2
    zz = lambda d: lax.rem(z + d + NZ, NZ)
    xx = lambda d: lax.rem(x + d + NX, NX)
    sib = {"row": r + 1 - 2 * k}
    ylp = {"row": r + 2 - 4 * yl}
    zp = {"row": lax.rem(r + 4, 32)}
    zm = {"row": lax.rem(r + 28, 32)}
    xp = {"col": lax.rem(c + 2, 8)}
    xm = {"col": lax.rem(c + 6, 8)}
    yhp = {"col": c + 1 - 2 * yh}

    barrier = pltpu.get_barrier_semaphore()
    for peer in (sib, ylp, zp, zm, xp, xm, yhp):
        pl.semaphore_signal(barrier, inc=1, device_id=peer, device_id_type=MESH)

    n_local = [0]
    local = {}

    def fetch(name, src, dst):
        copy = pltpu.make_async_copy(src, dst, loc_sem.at[n_local[0]])
        n_local[0] += 1
        copy.start()
        local[name] = copy

    fetch("grad", grad, grad_all.at[c])
    fetch("acts", acts, acts_all.at[c])
    fetch("g", gate, g_all.at[z, yl, k])
    fetch("u", up, u_all.at[z, yl, k])
    fetch("dw", dw, dw_v)
    fetch("gw", gw, gw_v)
    fetch("uw", uw, uw_v)
    pl.semaphore_wait(barrier, 7)

    copies = {}

    def send(name, src, dst, peer):
        i = len(copies)
        copy = pltpu.make_async_remote_copy(
            src_ref=src, dst_ref=dst, send_sem=send_sem.at[i], recv_sem=recv_sem.at[i],
            device_id=peer, device_id_type=MESH,
        )
        copy.start()
        copies[name] = copy

    def got(*names):
        for name in names:
            copies[name].wait_recv()

    class Col:
        def __init__(self, name, src, dst):
            self.n, self.src, self.dst = name, src, dst

        def s0(self):
            d = self.dst.at[c]
            send(self.n + "yh", self.src, d, yhp)
            send(self.n + "p0", self.src, d, xp)
            send(self.n + "m0", self.src, d, xm)

        def s1(self):
            got(self.n + "yh")
            d = self.dst.at[2 * x + 1 - yh]
            send(self.n + "p1", d, d, xp)
            send(self.n + "m1", d, d, xm)

        def s2(self):
            got(self.n + "p0")
            d = self.dst.at[2 * xx(-1) + yh]
            send(self.n + "p2", d, d, xp)

        def s3(self):
            got(self.n + "m1")
            d = self.dst.at[2 * xx(1) + 1 - yh]
            send(self.n + "m2", d, d, xm)

        def fin(self):
            got(self.n + "p1", self.n + "m0", self.n + "p2", self.n + "m2")

    class RowY:
        def __init__(self, name, src, piece, own=None):
            self.n, self.src, self.piece, self.own = name, src, piece, own

        def both(self, d):
            return self.piece(zz(d), slice(None), k)

        def s0(self):
            n, d = self.n, self.piece(z, yl, k)
            send(n + "y", self.src, d, ylp)
            send(n + "p0", self.src, d, zp)
            send(n + "m0", self.src, d, zm)

        def s1(self):
            n, d = self.n, self.piece(z, 1 - yl, k)
            got(n + "y")
            send(n + "p0o", d, d, zp)
            send(n + "m0o", d, d, zm)
            if self.own is not None:
                local[self.own].wait()
            send(n + "s0", self.both(0), self.both(0), sib)

        def hop(self, h):
            n = self.n
            tail = ("", "o") if h == 1 else ("",)
            got(*[n + "p" + str(h - 1) + t for t in tail])
            if h < 3:
                send(n + "p" + str(h), self.both(-h), self.both(-h), zp)
            else:
                d = self.piece(zz(-h), yl, k)
                send(n + "p3", d, d, zp)
            got(*[n + "m" + str(h - 1) + t for t in tail])
            if h < 3:
                send(n + "m" + str(h), self.both(h), self.both(h), zm)
            else:
                d = self.piece(zz(h), 1 - yl, k)
                send(n + "m3", d, d, zm)
            send(n + "sp" + str(h), self.both(-h), self.both(-h), sib)
            send(n + "sm" + str(h), self.both(h), self.both(h), sib)

        def last(self):
            n = self.n
            got(n + "p3", n + "m3")
            send(n + "s4", self.both(4), self.both(4), sib)

        def fin(self):
            n = self.n
            got(*[n + t for t in ("s0", "sp1", "sm1", "sp2", "sm2", "sp3", "sm3", "s4")])

    col_g = Col("cg", grad, grad_all)
    col_a = Col("ca", acts, acts_all)
    row_g = RowY("rg", gate, lambda a, b, e: g_all.at[a, b, e], "g")
    row_u = RowY("ru", up, lambda a, b, e: u_all.at[a, b, e], "u")

    col_g.s0()
    row_g.s0()
    row_u.s0()
    col_a.s0()
    col_g.s1()
    row_g.s1()
    row_u.s1()
    col_g.s2()
    col_g.s3()
    col_a.s1()
    row_g.hop(1)
    row_u.hop(1)
    local["grad"].wait()
    local["dw"].wait()
    col_g.fin()

    for j in range(CH):

        def tile(b, carry, j=j):
            left = grad_all[pl.ds(2 * b, 2)].reshape(256, 512)
            val = dot_nt(left, dw_v[j * W : (j + 1) * W, :])
            part[j, pl.ds(2 * b, 2)] = val.reshape(2, 2, 2, 32, W)
            return carry

        lax.fori_loop(0, 4, tile, 0)
        send("core" + str(j), part.at[j, :, :, 1 - k], rc.at[j], sib)

    col_a.s2()
    col_a.s3()
    row_g.hop(2)
    row_u.hop(2)

    for j in range(CH):
        got("core" + str(j))

        def add(b, carry, j=j):
            qb[j, b] = part[j, b, :, k] + rc[j, b]
            return carry

        lax.fori_loop(0, NZ, add, 0)

    for s in range(1, 5):
        for j in range(CH):
            for way in range(2):
                first = 1 if way == j % 2 else 2
                if s < first:
                    continue
                dest = zz(5 - s) if way == 0 else zz(s - 5)
                peer = zp if way == 0 else zm
                tag = "z%d%d" % (j, way)
                val = qb[j, dest]
                if s > first:
                    got(tag + str(s - 1))
                    val = val + zr[j, way, s - 2].astype(F32)
                if s < 4:
                    zs[j, way, s - 1] = val.astype(BF)
                    send(tag + str(s), zs.at[j, way, s - 1], zr.at[j, way, s - 1], peer)
                else:
                    zls[j, way] = val
                    send(tag + str(s), zls.at[j, way], zlr.at[j, way], peer)

    row_hg = []
    for j in range(CH):
        got("z%d04" % j, "z%d14" % j)
        sf[j] = qb[j, z] + zlr[j, 0] + zlr[j, 1]
        sb[j] = sf[j, 1 - yl].astype(BF)
        send("yl%d" % j, sb.at[j], ry.at[j], ylp)
    for j in range(CH):
        got("yl%d" % j)
        hg_all[j, z, yl, k] = (sf[j, yl] + ry[j].astype(F32)).astype(BF)
        own = hg_all.at[j, z, yl, k]
        flow = RowY("rh%d" % j, own, lambda a, b, e, j=j: hg_all.at[j, a, b, e])
        flow.s0()
        row_hg.append(flow)
    row_g.hop(3)
    row_u.hop(3)
    for flow in row_hg:
        flow.s1()
    row_g.last()
    row_u.last()
    for flow in row_hg:
        flow.hop(1)
    col_a.fin()
    row_g.fin()
    row_u.fin()

    def factors(b, carry):
        g = g_all[b].reshape(128, 1024).astype(F32)
        u = u_all[b].reshape(128, 1024).astype(F32)
        s = 0.5 * (1.0 + jnp.tanh(0.5 * g))
        swish = g * s
        hid[pl.ds(pl.multiple_of(b * 128, 128), 128), :] = (swish * u).astype(BF)
        a_f[b] = u * s * (1.0 + g * (1.0 - s))
        b_f[b] = swish
        return carry

    lax.fori_loop(0, 4, factors, 0)
    for flow in row_hg:
        flow.hop(2)
    lax.fori_loop(4, 8, factors, 0)
    for flow in row_hg:
        flow.hop(3)

    def down(n, carry):
        cols = pl.ds(pl.multiple_of(n * 256, 256), 256)
        down_v[cols, :] = dot_tn(hid[:, cols], grad_all[...].reshape(1024, 512)).astype(BF)
        return carry

    lax.fori_loop(0, 2, down, 0)
    for flow in row_hg:
        flow.last()
    lax.fori_loop(2, 4, down, 0)
    out_down = pltpu.make_async_copy(down_v, o_down, loc_sem.at[8])
    out_down.start()
    for flow in row_hg:
        flow.fin()
    local["gw"].wait()
    local["uw"].wait()
    local["acts"].wait()

    def block(xb):
        for e in range(2):
            b = 2 * xb + e
            for j in range(CH):
                cols = slice(j * W, (j + 1) * W)
                hg = hg_all[j, b].reshape(128, W).astype(F32)
                gb[b, :, cols] = (hg * a_f[b, :, cols]).astype(BF)
                ub[b, :, cols] = (hg * b_f[b, :, cols]).astype(BF)
        gbv = gb[pl.ds(2 * xb, 2)].reshape(256, 1024)
        ubv = ub[pl.ds(2 * xb, 2)].reshape(256, 1024)
        return dot_nt(gbv, gw_v[...]) + dot_nt(ubv, uw_v[...])

    val = block(xx(2))
    far_s[0] = val[:, :256].astype(BF)
    far_s[1] = val[:, 256:].astype(BF)
    send("fp", far_s.at[0], far_r.at[0], xp)
    send("fm", far_s.at[1], far_r.at[1], xm)
    val = block(xx(1))
    near_s[0, :, 256:] = val[:, 256:].astype(BF)
    got("fp")
    near_s[0, :, :256] = (val[:, :256] + far_r[0].astype(F32)).astype(BF)
    send("np", near_s.at[0], near_r.at[0], xp)
    val = block(xx(-1))
    near_s[1, :, :256] = val[:, :256].astype(BF)
    got("fm")
    near_s[1, :, 256:] = (val[:, 256:] + far_r[1].astype(F32)).astype(BF)
    send("nm", near_s.at[1], near_r.at[1], xm)
    own_f[...] = block(x).reshape(2, 128, 512)

    def weight(dst, src):
        def step(n, carry):
            cols = pl.ds(pl.multiple_of(n * 256, 256), 256)
            right = src[:, :, cols].reshape(1024, 256)
            dst[:, cols] = dot_tn(acts_all[...].reshape(1024, 512), right).astype(BF)
            return carry

        lax.fori_loop(0, 4, step, 0)

    weight(gate_v, gb)
    out_gate = pltpu.make_async_copy(gate_v, o_gate, loc_sem.at[9])
    out_gate.start()
    got("np", "nm")
    own_f[...] = (
        own_f[...]
        + near_r[0].astype(F32).reshape(2, 128, 512)
        + near_r[1].astype(F32).reshape(2, 128, 512)
    )
    ys[...] = own_f[1 - yh].astype(BF)
    send("yh", ys, yr, yhp)
    weight(up_v, ub)
    out_up = pltpu.make_async_copy(up_v, o_up, loc_sem.at[10])
    out_up.start()
    got("yh")
    in_v[...] = (own_f[yh] + yr[...].astype(F32)).astype(BF)
    out_in = pltpu.make_async_copy(in_v, o_in, loc_sem.at[11])
    out_in.start()
    for copy in copies.values():
        copy.wait_send()
    for copy in (out_down, out_gate, out_up, out_in):
        copy.wait()


def per_device(activations, out_grad, gate_pre, up_pre, gate_weight, up_weight, down_weight):
    hbm = pl.BlockSpec(memory_space=pl.ANY)
    outs = pl.pallas_call(
        kernel,
        out_shape=(
            jax.ShapeDtypeStruct((128, 512), BF),
            jax.ShapeDtypeStruct((512, 1024), BF),
            jax.ShapeDtypeStruct((512, 1024), BF),
            jax.ShapeDtypeStruct((1024, 512), BF),
        ),
        in_specs=[hbm] * 7,
        out_specs=(hbm,) * 4,
        scratch_shapes=[
            pltpu.VMEM((8, 128, 512), BF),
            pltpu.VMEM((8, 128, 512), BF),
            pltpu.VMEM((8, 2, 2, 32, 1024), BF),
            pltpu.VMEM((8, 2, 2, 32, 1024), BF),
            pltpu.VMEM((CH, 8, 2, 2, 32, W), BF),
            pltpu.VMEM((512, 1024), BF),
            pltpu.VMEM((512, 1024), BF),
            pltpu.VMEM((1024, 512), BF),
            pltpu.VMEM((CH, 8, 2, 2, 32, W), F32),
            pltpu.VMEM((CH, 8, 2, 32, W), F32),
            pltpu.VMEM((CH, 8, 2, 32, W), F32),
            pltpu.VMEM((CH, 2, 3, 2, 32, W), BF),
            pltpu.VMEM((CH, 2, 3, 2, 32, W), BF),
            pltpu.VMEM((CH, 2, 2, 32, W), F32),
            pltpu.VMEM((CH, 2, 2, 32, W), F32),
            pltpu.VMEM((CH, 2, 32, W), F32),
            pltpu.VMEM((CH, 32, W), BF),
            pltpu.VMEM((CH, 32, W), BF),
            pltpu.VMEM((8, 128, 1024), F32),
            pltpu.VMEM((8, 128, 1024), F32),
            pltpu.VMEM((1024, 1024), BF),
            pltpu.VMEM((8, 128, 1024), BF),
            pltpu.VMEM((8, 128, 1024), BF),
            pltpu.VMEM((2, 256, 256), BF),
            pltpu.VMEM((2, 256, 256), BF),
            pltpu.VMEM((2, 256, 512), BF),
            pltpu.VMEM((2, 256, 512), BF),
            pltpu.VMEM((2, 128, 512), F32),
            pltpu.VMEM((128, 512), BF),
            pltpu.VMEM((128, 512), BF),
            pltpu.VMEM((128, 512), BF),
            pltpu.VMEM((512, 1024), BF),
            pltpu.VMEM((512, 1024), BF),
            pltpu.VMEM((1024, 512), BF),
            pltpu.SemaphoreType.DMA((N_SEM,)),
            pltpu.SemaphoreType.DMA((N_SEM,)),
            pltpu.SemaphoreType.DMA((12,)),
        ],
        compiler_params=pltpu.CompilerParams(
            collective_id=0, has_side_effects=True, vmem_limit_bytes=60 * 1024 * 1024
        ),
    )(activations, out_grad, gate_pre, up_pre, gate_weight, up_weight, down_weight)
    return outs


def solution(mesh):
    placed = (
        P("col", "row"),
        P("col", "row"),
        P("row", "col"),
        P("row", "col"),
        P("row", "col"),
        P("row", "col"),
        P("col", "row"),
    )
    return jax.shard_map(
        per_device,
        mesh=mesh,
        in_specs=placed,
        out_specs=(P("col", "row"), P("row", "col"), P("row", "col"), P("col", "row")),
        check_vma=False,
    )
```

time: 539 us -> 99.4 us (0.18)
  waiting for transfers between devices: 495 us -> 0 us
  Pallas kernels: 0 us -> 91.6 us
  matrix products: 23.4 us -> 0 us
  between operations: 14.2 us -> 0.64 us
    all_gather x5 -> x0, waiting for transfers between devices: 291 us -> none  [the longest x1 65.6 us: per_device(): gate_piece = lax.all_gather(gate_back, 'row', axis=0, tiled=True)]
    reduce_scatter x2 -> x0, waiting for transfers between devices: 202 us -> none  [the longest x1 122 us: per_device(): lax.psum_scatter(contract_cols(grad_rows, down_weight), 'row', scatter_di...]
    pallas_call x0 -> x1, Pallas kernels: none -> 91.6 us  [per_device(): pl.pallas_call(kernel, out_shape=(jax.ShapeDtypeStruct((128, 512), BF), j...]
    dot_general x6 -> x0, matrix products: 23.4 us -> none  [the longest x3 13.6 us: contract_cols(): lax.dot_general(left, right, (((1,), (1,)), ((), ())), preferred_element_...]
  transfers between devices with their start and end apart: 7 -> 0, of which waited for: 7 -> 0; matrix products, arithmetic and copies ran while one was open for 4% -> 0% of each run, Pallas kernels for 0% -> 0%
where the time goes in v1:
time: 99.4 us; the launch traced here: 98.8 us
  Pallas kernels  91.6 us (92%)
  local copies, waits for them, and re-layouts  6.49 us (7%)
    pallas_call x1, Pallas kernels, per_device(): pl.pallas_call(kernel, out_shape=(jax.ShapeDtypeStruct((128, 512), BF), j...  91.6 us
    unnamed x8, local copies, waits for them, and re-layouts  6.49 us

profile of v1, /device:TPU:1, one launch (start us, length us, event | category | flops | bytes accessed | tf_op | source)
XLA Modules:
  0.0 98.8 jit_solution(15623334555002854464)
XLA Ops:
  0.6 91.6 %shard_map.102 = (bf16[128,512]{1,0:T(8,128)(2,1)}, bf16[512,1024]{1,0:T(8,128)(2,1)}, bf16[512,1024]{1,0:T(8,128)(2,1)}, bf16[1024,512]{1,0:T(8,128)(2,1)}) custom-call(bf16[128,512]{1,0:T(8,128)(2,1)} %acts.1, bf16[128,512]{1,0:T(8,128)(2,1)} %grad.1, bf16[32,1024]{1,0:T(8,128)(2,1)} %gate.1, bf16[32,1024]{1,0:T(8,128)(2,1)} %up.1, bf16[512,1024]{1,0:T(8,128)(2,1)} %gw.1, ...), custom_call_target="tpu_custom_call" | custom-call | tf_op jit(solution)/shard_map/pallas_call | solution.py:355
  92.3 1.6 %copy.15 = bf16[128,512]{1,0:T(8,128)(2,1)} copy(bf16[128,512]{1,0:T(8,128)(2,1)} %get-tuple-element.8) | data formatting | bytes 262144
  93.8 0.0 copy-start.1
  93.8 2.4 %copy.16 = bf16[512,1024]{1,0:T(8,128)(2,1)} copy(bf16[512,1024]{1,0:T(8,128)(2,1)} %get-tuple-element.9) | data formatting | bytes 2097152
  96.2 0.0 copy-done.1
  96.2 0.0 copy-start
  96.2 1.0 copy.17
  97.2 0.6 copy-done
  97.8 1.0 copy.18
Async XLA Ops:
  93.8 2.4 %copy-start.1 = (bf16[512,1024]{1,0:T(8,128)(2,1)S(1)}, bf16[512,1024]{1,0:T(8,128)(2,1)}, u32[]{:S(2)}) copy-start(bf16[512,1024]{1,0:T(8,128)(2,1)} %get-tuple-element.10) | copy-start | bytes 3145732
  96.2 1.6 %copy-start = (bf16[1024,512]{1,0:T(8,128)(2,1)S(1)}, bf16[1024,512]{1,0:T(8,128)(2,1)}, u32[]{:S(2)}) copy-start(bf16[1024,512]{1,0:T(8,128)(2,1)} %get-tuple-element.11) | copy-start | bytes 3145732

commit v2 on v1

v2 whole, which is shorter than its diff:
```python
import jax
import jax.numpy as jnp
from jax import lax
from jax.experimental import pallas as pl
from jax.experimental.pallas import tpu as pltpu
from jax.sharding import PartitionSpec as P

MESH = pl.DeviceIdType.MESH
BF = jnp.bfloat16
F32 = jnp.float32
NZ, NX = 8, 4
CH = 2
W = 1024 // CH
N_SEM = 192


def dot_nt(left, right):
    return lax.dot_general(left, right, (((1,), (1,)), ((), ())), preferred_element_type=F32)


def dot_tn(left, right):
    return lax.dot_general(left, right, (((0,), (0,)), ((), ())), preferred_element_type=F32)


def kernel(
    acts, grad, gate, up, gw, uw, dw,
    o_in, o_gate, o_up, o_down,
    acts_all, grad_all, g_all, u_all, hg_all, gw_v, uw_v, dw_v,
    part, rc, ys_r, yr_r, zs, zr, zls, zlr,
    a_f, b_f, hid, gb, ub,
    far_s, far_r, near_s, near_r, near_f, own_f, ys, yr,
    send_sem, recv_sem, loc_sem,
):
    r = lax.axis_index("row")
    c = lax.axis_index("col")
    k = lax.rem(r, 2)
    yl = lax.rem(r // 2, 2)
    z = r // 4
    yh = lax.rem(c, 2)
    x = c // 2
    zz = lambda d: lax.rem(z + d + NZ, NZ)
    xx = lambda d: lax.rem(x + d + NX, NX)
    sib = {"row": r + 1 - 2 * k}
    ylp = {"row": r + 2 - 4 * yl}
    zp = {"row": lax.rem(r + 4, 32)}
    zm = {"row": lax.rem(r + 28, 32)}
    xp = {"col": lax.rem(c + 2, 8)}
    xm = {"col": lax.rem(c + 6, 8)}
    yhp = {"col": c + 1 - 2 * yh}

    barrier = pltpu.get_barrier_semaphore()
    for peer in (sib, ylp, zp, zm, xp, xm, yhp):
        pl.semaphore_signal(barrier, inc=1, device_id=peer, device_id_type=MESH)

    n_local = [0]
    local = {}

    def fetch(name, src, dst):
        copy = pltpu.make_async_copy(src, dst, loc_sem.at[n_local[0]])
        n_local[0] += 1
        copy.start()
        local[name] = copy

    fetch("grad", grad, grad_all.at[c])
    fetch("acts", acts, acts_all.at[c])
    fetch("g", gate, g_all.at[z, yl, k])
    fetch("u", up, u_all.at[z, yl, k])
    fetch("dw", dw, dw_v)
    fetch("gw", gw, gw_v)
    fetch("uw", uw, uw_v)
    pl.semaphore_wait(barrier, 7)

    copies = {}

    def send(name, src, dst, peer):
        i = len(copies)
        copy = pltpu.make_async_remote_copy(
            src_ref=src, dst_ref=dst, send_sem=send_sem.at[i], recv_sem=recv_sem.at[i],
            device_id=peer, device_id_type=MESH,
        )
        copy.start()
        copies[name] = copy

    def got(*names):
        for name in names:
            copies[name].wait_recv()

    rows64 = (slice(0, 64), slice(64, 128))

    class Col:
        def __init__(self, name, src, dst):
            self.n, self.src, self.dst = name, src, dst

        def s0(self):
            d = self.dst.at[c]
            send(self.n + "yh", self.src, d, yhp)
            send(self.n + "p0", self.src, d, xp)
            send(self.n + "m0", self.src, d, xm)

        def s1(self):
            got(self.n + "yh")
            d = self.dst.at[2 * x + 1 - yh]
            send(self.n + "p1", d, d, xp)
            send(self.n + "m1", d, d, xm)

        def s2(self):
            got(self.n + "p0")
            d = self.dst.at[2 * xx(-1) + yh]
            send(self.n + "p2", d, d, xp)

        def s3(self):
            got(self.n + "m1")
            d = self.dst.at[2 * xx(1) + 1 - yh]
            send(self.n + "m2", d, d, xm)

        def fin(self):
            got(self.n + "p1", self.n + "m0", self.n + "p2", self.n + "m2")

    class ColFast:
        def __init__(self, name, src, dst):
            self.n, self.src, self.dst = name, src, dst

        def s0(self):
            for h in range(2):
                send(self.n + "yh%d" % h, self.src.at[rows64[h]], self.dst.at[c, rows64[h]], yhp)
                send(self.n + "p0%d" % h, self.src.at[rows64[h]], self.dst.at[c, rows64[h]], xp)
                g = 1 - h
                send(self.n + "m0%d" % g, self.src.at[rows64[g]], self.dst.at[c, rows64[g]], xm)

        def s1(self, h):
            got(self.n + "yh%d" % h)
            d = self.dst.at[2 * x + 1 - yh, rows64[h]]
            send(self.n + "p1%d" % h, d, d, xp)
            send(self.n + "m1%d" % h, d, d, xm)

        def s2(self):
            got(self.n + "p00", self.n + "m01")
            d = self.dst.at[2 * xx(-1) + yh, rows64[0]]
            send(self.n + "p2", d, d, xp)
            d = self.dst.at[2 * xx(1) + yh, rows64[1]]
            send(self.n + "m2", d, d, xm)

        def s3(self):
            got(self.n + "p10")
            d = self.dst.at[2 * xx(-1) + 1 - yh, rows64[0]]
            send(self.n + "p3", d, d, xp)
            got(self.n + "m11")
            d = self.dst.at[2 * xx(1) + 1 - yh, rows64[1]]
            send(self.n + "m3", d, d, xm)

    class RowY:
        def __init__(self, name, src, piece, own=None):
            self.n, self.src, self.piece, self.own = name, src, piece, own

        def both(self, d):
            return self.piece(zz(d), slice(None), k)

        def s0(self):
            n, d = self.n, self.piece(z, yl, k)
            send(n + "y", self.src, d, ylp)
            send(n + "p0", self.src, d, zp)
            send(n + "m0", self.src, d, zm)

        def s1(self):
            n, d = self.n, self.piece(z, 1 - yl, k)
            got(n + "y")
            send(n + "p0o", d, d, zp)
            send(n + "m0o", d, d, zm)
            if self.own is not None:
                local[self.own].wait()
            send(n + "s0", self.both(0), self.both(0), sib)

        def hop(self, h):
            n = self.n
            tail = ("", "o") if h == 1 else ("",)
            got(*[n + "p" + str(h - 1) + t for t in tail])
            if h < 3:
                send(n + "p" + str(h), self.both(-h), self.both(-h), zp)
            else:
                d = self.piece(zz(-h), yl, k)
                send(n + "p3", d, d, zp)
            got(*[n + "m" + str(h - 1) + t for t in tail])
            if h < 3:
                send(n + "m" + str(h), self.both(h), self.both(h), zm)
            else:
                d = self.piece(zz(h), 1 - yl, k)
                send(n + "m3", d, d, zm)
            send(n + "sp" + str(h), self.both(-h), self.both(-h), sib)
            send(n + "sm" + str(h), self.both(h), self.both(h), sib)

        def last(self):
            n = self.n
            got(n + "p3", n + "m3")
            send(n + "s4", self.both(4), self.both(4), sib)

        def fin(self):
            n = self.n
            got(*[n + t for t in ("s0", "sp1", "sm1", "sp2", "sm2", "sp3", "sm3", "s4")])

    halves = [slice(j * W, (j + 1) * W) for j in range(CH)]

    class RowL:
        def __init__(self, name, ref, cols, src=None, own=None):
            self.n, self.ref, self.cols, self.src, self.own = name, ref, cols, src, own

        def pair(self, tag, d):
            at = self.ref.at[zz(d), yl, k]
            send(self.n + "y" + tag, at if self.src is None or d else self.src, at, ylp)

        def s0(self):
            for j, cols in enumerate(self.cols):
                d = self.ref.at[z, yl, k, :, cols]
                src = d if self.src is None else self.src.at[:, cols]
                send(self.n + "p0%d" % j, src, d, zp)
                send(self.n + "m0%d" % j, src, d, zm)

        def s1(self):
            self.pair("p0", 0)

        def hop(self, h):
            for way, to, sign in (("p", zp, -1), ("m", zm, 1)):
                for j, cols in enumerate(self.cols):
                    got("%s%s%d%d" % (self.n, way, h - 1, j))
                    if h < 3 or (way == "p") == (j == 0):
                        d = self.ref.at[zz(sign * h), yl, k, :, cols]
                        send("%s%s%d%d" % (self.n, way, h, j), d, d, to)
                self.pair("%s%d" % (way, h), sign * h)

        def last(self):
            for j in range(len(self.cols)):
                got(self.n + ("p30", "m31")[j])
            self.pair("p4", 4)

        def core(self, h):
            if h == 0 and self.own is not None:
                local[self.own].wait()
            for way, sign in (("p", -1), ("m", 1)):
                if way == "m" and h in (0, 4):
                    continue
                got("%sy%s%d" % (self.n, way, h))
                d = self.ref.at[zz(sign * h), :, k]
                send("%ss%s%d" % (self.n, way, h), d, d, sib)

        def fin(self):
            got(*[self.n + "sp%d" % h for h in range(5)])
            got(*[self.n + "sm%d" % h for h in range(1, 4)])

    col_g = ColFast("cg", grad, grad_all)
    col_a = Col("ca", acts, acts_all)
    row_g = RowY("rg", gate, lambda a, b, e: g_all.at[a, b, e], "g")
    row_u = RowL("ru", u_all, [slice(0, 1024)], up, "u")

    def partial(xb, tag):
        left = grad_all[pl.ds(2 * xb, 2)].reshape(256, 512)
        for j in range(CH):
            val = dot_nt(left, dw_v[j * W : (j + 1) * W, :])
            part[pl.ds(2 * xb, 2), :, :, :, halves[j]] = val.reshape(2, 2, 2, 32, W)
        send("core" + tag, part.at[pl.ds(2 * xb, 2), :, 1 - k], rc.at[pl.ds(2 * xb, 2)], sib)

    col_g.s0()
    row_g.s0()
    row_u.s0()
    col_g.s2()
    col_g.s1(0)
    col_g.s1(1)
    row_u.s1()
    row_g.s1()
    row_u.hop(1)
    local["grad"].wait()
    local["dw"].wait()
    partial(x, "0")
    row_u.core(0)
    col_g.s3()
    row_g.hop(1)
    row_u.hop(2)
    got("cgp01", "cgp11")
    partial(xx(-1), "p")
    got("cgm00", "cgm10")
    partial(xx(1), "m")
    row_u.core(1)
    row_u.hop(3)
    got("cgp2", "cgm2", "cgp3", "cgm3")
    partial(xx(2), "f")
    col_a.s0()
    got("core0", "corep", "corem", "coref")

    order = (4, 3, 5, 2, 6, 1, 7, 0)
    for d in order:
        b = zz(d)
        ys_r[d] = (part[b, 1 - yl, k] + rc[b, 1 - yl]).astype(BF)
        send("y%d" % d, ys_r.at[d], yr_r.at[d], ylp)

    def mine(d, cols):
        b = zz(d)
        return part[b, yl, k, :, cols] + rc[b, yl, :, cols] + yr_r[d, :, cols].astype(F32)

    for s in range(1, 5):
        if s == 1:
            got("y4")
        else:
            got("y%d" % (5 - s), "y%d" % (3 + s))
        for way in range(2):
            for j in range(CH):
                first = 1 if way == j else 2
                if s < first:
                    continue
                d = 5 - s if way == 0 else 3 + s
                peer = zp if way == 0 else zm
                tag = "z%d%d" % (j, way)
                val = mine(d, halves[j])
                if s > first:
                    got(tag + str(s - 1))
                    val = val + zr[j, way, s - 2].astype(F32)
                if s < 4:
                    zs[j, way, s - 1] = val.astype(BF)
                    send(tag + str(s), zs.at[j, way, s - 1], zr.at[j, way, s - 1], peer)
                else:
                    zls[j, way] = val
                    send(tag + str(s), zls.at[j, way], zlr.at[j, way], peer)
        if s == 1:
            row_g.hop(2)
            col_a.s1()
        if s == 2:
            row_u.core(2)
            row_u.last()
            col_a.s2()
            col_a.s3()
        if s == 3:
            row_g.hop(3)
            row_u.core(3)

    row_u.core(4)
    row_g.last()
    panel = RowL("rh", hg_all, halves)
    got("y0")
    for j in range(CH):
        got("z%d04" % j, "z%d14" % j)
        hg_all[z, yl, k, :, halves[j]] = (mine(0, halves[j]) + zlr[j, 0] + zlr[j, 1]).astype(BF)
    panel.s0()
    panel.s1()
    row_g.fin()
    row_u.fin()

    def factors(b, carry):
        g = g_all[b].reshape(128, 1024).astype(F32)
        u = u_all[b].reshape(128, 1024).astype(F32)
        s = 0.5 * (1.0 + jnp.tanh(0.5 * g))
        swish = g * s
        hid[pl.ds(pl.multiple_of(b * 128, 128), 128), :] = (swish * u).astype(BF)
        a_f[b] = u * s * (1.0 + g * (1.0 - s))
        b_f[b] = swish
        return carry

    lax.fori_loop(0, 4, factors, 0)
    panel.hop(1)
    panel.core(0)
    lax.fori_loop(4, 8, factors, 0)
    panel.hop(2)
    panel.core(1)

    def down(n, carry):
        cols = pl.ds(pl.multiple_of(n * 256, 256), 256)
        o_down[cols, :] = dot_tn(hid[:, cols], grad_all[...].reshape(1024, 512)).astype(BF)
        return carry

    lax.fori_loop(0, 2, down, 0)
    panel.hop(3)
    panel.core(2)
    panel.last()
    panel.core(3)
    lax.fori_loop(2, 4, down, 0)
    panel.core(4)
    col_a.fin()
    panel.fin()
    local["gw"].wait()
    local["uw"].wait()
    local["acts"].wait()

    def derive(xb):
        for e in range(2):
            b = 2 * xb + e
            hg = hg_all[b].reshape(128, 1024).astype(F32)
            gb[b] = (hg * a_f[b]).astype(BF)
            ub[b] = (hg * b_f[b]).astype(BF)

    def block(xb, side):
        gbv = gb[pl.ds(2 * xb, 2)].reshape(256, 1024)
        ubv = ub[pl.ds(2 * xb, 2)].reshape(256, 1024)
        rows = slice(256 * side, 256 * side + 256)
        return dot_nt(gbv, gw_v[rows, :]) + dot_nt(ubv, uw_v[rows, :])

    first, second = 1 - yh, yh
    derive(xx(2))
    far_s[0] = block(xx(2), 0).astype(BF).reshape(2, 128, 256)
    send("fp0", far_s.at[0, first], far_r.at[0, first], xp)
    far_s[1] = block(xx(2), 1).astype(BF).reshape(2, 128, 256)
    send("fm0", far_s.at[1, first], far_r.at[1, first], xm)
    derive(xx(1))
    near_s[0, 1] = block(xx(1), 1).astype(BF).reshape(2, 128, 256)
    send("np10", near_s.at[0, 1, first], near_r.at[0, 1, first], xp)
    send("fp1", far_s.at[0, second], far_r.at[0, second], xp)
    derive(xx(-1))
    near_s[1, 0] = block(xx(-1), 0).astype(BF).reshape(2, 128, 256)
    send("nm00", near_s.at[1, 0, first], near_r.at[1, 0, first], xm)
    send("fm1", far_s.at[1, second], far_r.at[1, second], xm)
    near_f[0] = block(xx(1), 0).reshape(2, 128, 256)
    got("fp0")
    near_s[0, 0, first] = (near_f[0, first] + far_r[0, first].astype(F32)).astype(BF)
    send("np00", near_s.at[0, 0, first], near_r.at[0, 0, first], xp)
    send("np11", near_s.at[0, 1, second], near_r.at[0, 1, second], xp)
    near_f[1] = block(xx(-1), 1).reshape(2, 128, 256)
    got("fm0")
    near_s[1, 1, first] = (near_f[1, first] + far_r[1, first].astype(F32)).astype(BF)
    send("nm10", near_s.at[1, 1, first], near_r.at[1, 1, first], xm)
    send("nm01", near_s.at[1, 0, second], near_r.at[1, 0, second], xm)
    got("fp1")
    near_s[0, 0, second] = (near_f[0, second] + far_r[0, second].astype(F32)).astype(BF)
    send("np01", near_s.at[0, 0, second], near_r.at[0, 0, second], xp)
    got("fm1")
    near_s[1, 1, second] = (near_f[1, second] + far_r[1, second].astype(F32)).astype(BF)
    send("nm11", near_s.at[1, 1, second], near_r.at[1, 1, second], xm)
    derive(x)
    for side in range(2):
        own_f[side] = block(x, side).reshape(2, 128, 256)

    def total(side, e, part_of):
        got("np%d%d" % (side, part_of), "nm%d%d" % (side, part_of))
        near = near_r[0, side, e].astype(F32) + near_r[1, side, e].astype(F32)
        return own_f[side, e] + near

    for side in range(2):
        ys[side] = total(side, first, 0).astype(BF)
        send("yh%d" % side, ys.at[side], yr.at[side], yhp)

    def weight(dst, src):
        def step(n, carry):
            cols = pl.ds(pl.multiple_of(n * 256, 256), 256)
            right = src[:, :, cols].reshape(1024, 256)
            dst[:, cols] = dot_tn(acts_all[...].reshape(1024, 512), right).astype(BF)
            return carry

        lax.fori_loop(0, 4, step, 0)

    weight(o_gate, gb)
    weight(o_up, ub)
    for side in range(2):
        val = total(side, second, 1)
        got("yh%d" % side)
        o_in[:, 256 * side : 256 * side + 256] = (val + yr[side].astype(F32)).astype(BF)
    for copy in copies.values():
        copy.wait_send()


def leave(*refs):
    sems = refs[-1]
    copies = [pltpu.make_async_copy(refs[i], refs[4 + i], sems.at[i]) for i in range(4)]
    for copy in copies:
        copy.start()
    for copy in copies:
        copy.wait()


def per_device(activations, out_grad, gate_pre, up_pre, gate_weight, up_weight, down_weight):
    hbm = pl.BlockSpec(memory_space=pl.ANY)
    outs = pl.pallas_call(
        kernel,
        out_shape=(
            pltpu.VMEM((128, 512), BF),
            pltpu.VMEM((512, 1024), BF),
            pltpu.VMEM((512, 1024), BF),
            pltpu.VMEM((1024, 512), BF),
        ),
        in_specs=[hbm] * 7,
        out_specs=(pl.BlockSpec(memory_space=pltpu.VMEM),) * 4,
        scratch_shapes=[
            pltpu.VMEM((8, 128, 512), BF),
            pltpu.VMEM((8, 128, 512), BF),
            pltpu.VMEM((8, 2, 2, 32, 1024), BF),
            pltpu.VMEM((8, 2, 2, 32, 1024), BF),
            pltpu.VMEM((8, 2, 2, 32, 1024), BF),
            pltpu.VMEM((512, 1024), BF),
            pltpu.VMEM((512, 1024), BF),
            pltpu.VMEM((1024, 512), BF),
            pltpu.VMEM((8, 2, 2, 32, 1024), F32),
            pltpu.VMEM((8, 2, 32, 1024), F32),
            pltpu.VMEM((8, 32, 1024), BF),
            pltpu.VMEM((8, 32, 1024), BF),
            pltpu.VMEM((CH, 2, 3, 32, W), BF),
            pltpu.VMEM((CH, 2, 3, 32, W), BF),
            pltpu.VMEM((CH, 2, 32, W), F32),
            pltpu.VMEM((CH, 2, 32, W), F32),
            pltpu.VMEM((8, 128, 1024), F32),
            pltpu.VMEM((8, 128, 1024), F32),
            pltpu.VMEM((1024, 1024), BF),
            pltpu.VMEM((8, 128, 1024), BF),
            pltpu.VMEM((8, 128, 1024), BF),
            pltpu.VMEM((2, 2, 128, 256), BF),
            pltpu.VMEM((2, 2, 128, 256), BF),
            pltpu.VMEM((2, 2, 2, 128, 256), BF),
            pltpu.VMEM((2, 2, 2, 128, 256), BF),
            pltpu.VMEM((2, 2, 128, 256), F32),
            pltpu.VMEM((2, 2, 128, 256), F32),
            pltpu.VMEM((2, 128, 256), BF),
            pltpu.VMEM((2, 128, 256), BF),
            pltpu.SemaphoreType.DMA((N_SEM,)),
            pltpu.SemaphoreType.DMA((N_SEM,)),
            pltpu.SemaphoreType.DMA((12,)),
        ],
        compiler_params=pltpu.CompilerParams(
            collective_id=0, has_side_effects=True, vmem_limit_bytes=56 * 1024 * 1024
        ),
    )(activations, out_grad, gate_pre, up_pre, gate_weight, up_weight, down_weight)
    return pl.pallas_call(
        leave,
        out_shape=tuple(jax.ShapeDtypeStruct(o.shape, BF) for o in outs),
        in_specs=[hbm] * 4,
        out_specs=(hbm,) * 4,
        scratch_shapes=[pltpu.SemaphoreType.DMA((4,))],
        compiler_params=pltpu.CompilerParams(vmem_limit_bytes=1024 * 1024),
    )(*outs)


def solution(mesh):
    placed = (
        P("col", "row"),
        P("col", "row"),
        P("row", "col"),
        P("row", "col"),
        P("row", "col"),
        P("row", "col"),
        P("col", "row"),
    )
    return jax.shard_map(
        per_device,
        mesh=mesh,
        in_specs=placed,
        out_specs=(P("col", "row"), P("row", "col"), P("row", "col"), P("col", "row")),
        check_vma=False,
    )
```

time: 99.4 us -> 86.5 us (0.87)
  local copies, waits for them, and re-layouts: 6.49 us -> 0 us
  Pallas kernels: 91.6 us -> 85.7 us
    unnamed x8 -> x0, local copies, waits for them, and re-layouts: 6.49 us -> none
    pallas_call x1 -> x2, Pallas kernels: 91.6 us -> 85.7 us  [the longest x1 84 us: per_device(): pl.pallas_call(kernel, out_shape=(pltpu.VMEM((128, 512), BF), pltpu.VMEM(...]
where the time goes in v2:
time: 86.5 us; the launch traced here: 86.4 us
  Pallas kernels  85.7 us (99%)
    pallas_call x1, Pallas kernels, per_device(): pl.pallas_call(kernel, out_shape=(pltpu.VMEM((128, 512), BF), pltpu.VMEM(...  84 us
    pallas_call x1, Pallas kernels, per_device(): pl.pallas_call(leave, out_shape=tuple((jax.ShapeDtypeStruct(o.shape, BF)...  1.74 us

profile of v2, /device:TPU:1, one launch (start us, length us, event | category | flops | bytes accessed | tf_op | source)
XLA Modules:
  0.0 86.4 jit_solution(6510270024083116256)
XLA Ops:
  0.6 84.0 %shard_map.102 = (bf16[128,512]{1,0:T(8,128)(2,1)S(1)}, bf16[512,1024]{1,0:T(8,128)(2,1)S(1)}, bf16[512,1024]{1,0:T(8,128)(2,1)S(1)}, bf16[1024,512]{1,0:T(8,128)(2,1)S(1)}) custom-call(bf16[128,512]{1,0:T(8,128)(2,1)} %acts.1, bf16[128,512]{1,0:T(8,128)(2,1)} %grad.1, bf16[32,1024]{1,0:T(8,128)(2,1)} %gate.1, bf16[32,1024]{1,0:T(8,128)(2,1)} %up.1, ...), custom_call_target="tpu_custom_call" | custom-call | tf_op jit(solution)/shard_map/pallas_call | solution.py:465
  84.6 1.7 %shard_map.103 = (bf16[128,512]{1,0:T(8,128)(2,1)}, bf16[512,1024]{1,0:T(8,128)(2,1)}, bf16[512,1024]{1,0:T(8,128)(2,1)}, bf16[1024,512]{1,0:T(8,128)(2,1)}) custom-call(bf16[128,512]{1,0:T(8,128)(2,1)S(1)} %get-tuple-element.8.refs_0_, bf16[512,1024]{1,0:T(8,128)(2,1)S(1)} %get-tuple-element.9.refs_1_, bf16[512,1024]{1,0:T(8,128)(2,1)S(1)} %get-tuple-element.10.refs_2_, ...), custom_call_target="tpu_custom_call" | custom-call | tf_op jit(solution)/shard_map/pallas_call | solution.py:513

commit v3 on v2

--- a/solution.py
+++ b/solution.py
@@ -26,7 +26,7 @@
     acts, grad, gate, up, gw, uw, dw,
     o_in, o_gate, o_up, o_down,
     acts_all, grad_all, g_all, u_all, hg_all, gw_v, uw_v, dw_v,
-    part, rc, ys_r, yr_r, zs, zr, zls, zlr,
+    part, rc, ys_r, yr_r, far_zs, far_zr, zs, zr,
     a_f, b_f, hid, gb, ub,
     far_s, far_r, near_s, near_r, near_f, own_f, ys, yr,
     send_sem, recv_sem, loc_sem,
@@ -44,12 +44,14 @@
     ylp = {"row": r + 2 - 4 * yl}
     zp = {"row": lax.rem(r + 4, 32)}
     zm = {"row": lax.rem(r + 28, 32)}
+    zp2 = {"row": lax.rem(r + 8, 32)}
+    zm2 = {"row": lax.rem(r + 24, 32)}
     xp = {"col": lax.rem(c + 2, 8)}
     xm = {"col": lax.rem(c + 6, 8)}
     yhp = {"col": c + 1 - 2 * yh}
 
     barrier = pltpu.get_barrier_semaphore()
-    for peer in (sib, ylp, zp, zm, xp, xm, yhp):
+    for peer in (sib, ylp, zp, zm, zp2, zm2, xp, xm, yhp):
         pl.semaphore_signal(barrier, inc=1, device_id=peer, device_id_type=MESH)
 
     n_local = [0]
@@ -68,7 +70,7 @@
     fetch("dw", dw, dw_v)
     fetch("gw", gw, gw_v)
     fetch("uw", uw, uw_v)
-    pl.semaphore_wait(barrier, 7)
+    pl.semaphore_wait(barrier, 9)
 
     copies = {}
 
@@ -217,13 +219,16 @@
         def s1(self):
             self.pair("p0", 0)
 
-        def hop(self, h):
+        def hop_z(self, h):
             for way, to, sign in (("p", zp, -1), ("m", zm, 1)):
                 for j, cols in enumerate(self.cols):
                     got("%s%s%d%d" % (self.n, way, h - 1, j))
                     if h < 3 or (way == "p") == (j == 0):
                         d = self.ref.at[zz(sign * h), yl, k, :, cols]
                         send("%s%s%d%d" % (self.n, way, h, j), d, d, to)
+
+        def pairs(self, h):
+            for way, sign in (("p", -1), ("m", 1)):
                 self.pair("%s%d" % (way, h), sign * h)
 
         def last(self):
@@ -245,6 +250,42 @@
             got(*[self.n + "sp%d" % h for h in range(5)])
             got(*[self.n + "sm%d" % h for h in range(1, 4)])
 
+    class Panel:
+        def at(self, d, j):
+            return hg_all.at[zz(d), yl, k, :, halves[j]]
+
+        def s0(self):
+            for j in range(CH):
+                for name, to in (("2p", zp2), ("2m", zm2), ("1p", zp), ("1m", zm)):
+                    send("h%s%d" % (name, j), self.at(0, j), self.at(0, j), to)
+            for j in range(CH):
+                self.pair(0, j)
+
+        def pair(self, d, j):
+            send("hy%d%d" % (d, j), self.at(d, j), self.at(d, j), ylp)
+
+        def relay(self, j):
+            for way, d, to, on in (("p", -2, zp, zp2), ("m", 2, zm, zm2)):
+                got("h2%s%d" % (way, j))
+                at = self.at(d, j)
+                send("h3%s%d" % (way, j), at, at, to)
+                if (way == "p") == (j == 0):
+                    send("h4%s%d" % (way, j), at, at, on)
+                self.pair(d, j)
+
+        def take(self, name, j, d):
+            got("h%s%d" % (name, j))
+            self.pair(d, j)
+
+        def core(self, *ds):
+            for d in ds:
+                got("hy%d0" % d, "hy%d1" % d)
+                at = hg_all.at[zz(d), :, k]
+                send("hs%d" % d, at, at, sib)
+
+        def fin(self):
+            got(*["hs%d" % d for d in (0, -1, 1, -2, 2, -3, 3, 4)])
+
     col_g = ColFast("cg", grad, grad_all)
     col_a = Col("ca", acts, acts_all)
     row_g = RowY("rg", gate, lambda a, b, e: g_all.at[a, b, e], "g")
@@ -258,88 +299,91 @@
         send("core" + tag, part.at[pl.ds(2 * xb, 2), :, 1 - k], rc.at[pl.ds(2 * xb, 2)], sib)
 
     col_g.s0()
+    row_u.s0()
     row_g.s0()
-    row_u.s0()
     col_g.s2()
     col_g.s1(0)
     col_g.s1(1)
     row_u.s1()
     row_g.s1()
-    row_u.hop(1)
+    row_u.hop_z(1)
+    row_u.pairs(1)
     local["grad"].wait()
     local["dw"].wait()
     partial(x, "0")
-    row_u.core(0)
     col_g.s3()
-    row_g.hop(1)
-    row_u.hop(2)
     got("cgp01", "cgp11")
     partial(xx(-1), "p")
     got("cgm00", "cgm10")
     partial(xx(1), "m")
-    row_u.core(1)
-    row_u.hop(3)
+    row_u.hop_z(2)
+    row_u.pairs(2)
+    row_g.hop(1)
     got("cgp2", "cgm2", "cgp3", "cgm3")
     partial(xx(2), "f")
+    got("core0", "corep", "corem", "coref")
+
+    def give(d, j):
+        b, cols = zz(d), halves[j]
+        ys_r[d, :, cols] = (part[b, 1 - yl, k, :, cols] + rc[b, 1 - yl, :, cols]).astype(BF)
+        send("y%d%d" % (d, j), ys_r.at[d, :, cols], yr_r.at[d, :, cols], ylp)
+
+    for d, j in ((4, 0), (4, 1), (3, 0), (5, 0), (3, 1), (5, 1), (2, 0), (6, 0), (2, 1), (6, 1)):
+        give(d, j)
+    for d in (1, 7, 0):
+        give(d, 0)
+        give(d, 1)
+
+    def mine(d, j):
+        b, cols = zz(d), halves[j]
+        got("y%d%d" % (d, j))
+        return part[b, yl, k, :, cols] + rc[b, yl, :, cols] + yr_r[d, :, cols].astype(F32)
+
+    def hand(stage, way, j, val, peer):
+        zs[stage, way, :, halves[j]] = val.astype(BF)
+        at = (stage, way, slice(None), halves[j])
+        send("z%d%d%d" % (stage, way, j), zs.at[at], zr.at[at], peer)
+
+    for way, peer in enumerate((zp2, zm2)):
+        far_zs[way] = mine(4, way).astype(BF)
+        send("z4%d" % way, far_zs.at[way], far_zr.at[way], peer)
+    for j in range(CH):
+        for way, d, peer in ((0, 3, zp), (1, 5, zm)):
+            hand(0, way, j, mine(d, j), peer)
     col_a.s0()
-    got("core0", "corep", "corem", "coref")
-
-    order = (4, 3, 5, 2, 6, 1, 7, 0)
-    for d in order:
-        b = zz(d)
-        ys_r[d] = (part[b, 1 - yl, k] + rc[b, 1 - yl]).astype(BF)
-        send("y%d" % d, ys_r.at[d], yr_r.at[d], ylp)
-
-    def mine(d, cols):
-        b = zz(d)
-        return part[b, yl, k, :, cols] + rc[b, yl, :, cols] + yr_r[d, :, cols].astype(F32)
-
-    for s in range(1, 5):
-        if s == 1:
-            got("y4")
-        else:
-            got("y%d" % (5 - s), "y%d" % (3 + s))
-        for way in range(2):
-            for j in range(CH):
-                first = 1 if way == j else 2
-                if s < first:
-                    continue
-                d = 5 - s if way == 0 else 3 + s
-                peer = zp if way == 0 else zm
-                tag = "z%d%d" % (j, way)
-                val = mine(d, halves[j])
-                if s > first:
-                    got(tag + str(s - 1))
-                    val = val + zr[j, way, s - 2].astype(F32)
-                if s < 4:
-                    zs[j, way, s - 1] = val.astype(BF)
-                    send(tag + str(s), zs.at[j, way, s - 1], zr.at[j, way, s - 1], peer)
-                else:
-                    zls[j, way] = val
-                    send(tag + str(s), zls.at[j, way], zlr.at[j, way], peer)
-        if s == 1:
-            row_g.hop(2)
-            col_a.s1()
-        if s == 2:
-            row_u.core(2)
-            row_u.last()
-            col_a.s2()
-            col_a.s3()
-        if s == 3:
-            row_g.hop(3)
-            row_u.core(3)
-
-    row_u.core(4)
-    row_g.last()
-    panel = RowL("rh", hg_all, halves)
-    got("y0")
+    row_u.core(0)
+    row_u.core(1)
     for j in range(CH):
-        got("z%d04" % j, "z%d14" % j)
-        hg_all[z, yl, k, :, halves[j]] = (mine(0, halves[j]) + zlr[j, 0] + zlr[j, 1]).astype(BF)
+        for way, d, peer in ((0, 2, zp2), (1, 6, zm2)):
+            val = mine(d, j)
+            got("z0%d%d" % (way, j))
+            val = val + zr[0, way, :, halves[j]].astype(F32)
+            if way == j:
+                got("z4%d" % way)
+                val = val + far_zr[way].astype(F32)
+            hand(1, way, j, val, peer)
+    for j in range(CH):
+        for way, d, peer in ((0, 1, zp), (1, 7, zm)):
+            hand(2, way, j, mine(d, j), peer)
+    row_u.hop_z(3)
+    row_u.pairs(3)
+    row_g.hop(2)
+    col_a.s1()
+    row_u.core(2)
+    for j in range(CH):
+        val = mine(0, j)
+        for stage in (2, 1):
+            for way in range(2):
+                got("z%d%d%d" % (stage, way, j))
+                val = val + zr[stage, way, :, halves[j]].astype(F32)
+        hg_all[z, yl, k, :, halves[j]] = val.astype(BF)
+    panel = Panel()
     panel.s0()
-    panel.s1()
-    row_g.fin()
-    row_u.fin()
+    row_u.last()
+    row_g.hop(3)
+    row_u.core(3)
+    col_a.s2()
+    col_a.s3()
 
     def factors(b, carry):
         g = g_all[b].reshape(128, 1024).astype(F32)
@@ -351,25 +395,33 @@
         b_f[b] = swish
         return carry
 
-    lax.fori_loop(0, 4, factors, 0)
-    panel.hop(1)
+    panel.relay(0)
+    panel.relay(1)
+    for j in range(CH):
+        panel.take("1p", j, -1)
+        panel.take("1m", j, 1)
+    row_u.core(4)
+    row_g.last()
     panel.core(0)
-    lax.fori_loop(4, 8, factors, 0)
-    panel.hop(2)
-    panel.core(1)
+    row_u.fin()
+    row_g.fin()
+    lax.fori_loop(0, 3, factors, 0)
 
     def down(n, carry):
         cols = pl.ds(pl.multiple_of(n * 256, 256), 256)
         o_down[cols, :] = dot_tn(hid[:, cols], grad_all[...].reshape(1024, 512)).astype(BF)
         return carry
 
-    lax.fori_loop(0, 2, down, 0)
-    panel.hop(3)
-    panel.core(2)
-    panel.last()
-    panel.core(3)
-    lax.fori_loop(2, 4, down, 0)
-    panel.core(4)
+    panel.take("4p", 0, 4)
+    for j in range(CH):
+        panel.take("3p", j, -3)
+        panel.take("3m", j, 3)
+    panel.take("4m", 1, 4)
+    panel.core(-2, 2)
+    lax.fori_loop(3, 8, factors, 0)
+    panel.core(-1, 1)
+    lax.fori_loop(0, 4, down, 0)
+    panel.core(-3, 3, 4)
     col_a.fin()
     panel.fin()
     local["gw"].wait()
@@ -485,10 +537,10 @@
             pltpu.VMEM((8, 2, 32, 1024), F32),
             pltpu.VMEM((8, 32, 1024), BF),
             pltpu.VMEM((8, 32, 1024), BF),
-            pltpu.VMEM((CH, 2, 3, 32, W), BF),
-            pltpu.VMEM((CH, 2, 3, 32, W), BF),
-            pltpu.VMEM((CH, 2, 32, W), F32),
-            pltpu.VMEM((CH, 2, 32, W), F32),
+            pltpu.VMEM((2, 32, W), BF),
+            pltpu.VMEM((2, 32, W), BF),
+            pltpu.VMEM((3, 2, 32, 1024), BF),
+            pltpu.VMEM((3, 2, 32, 1024), BF),
             pltpu.VMEM((8, 128, 1024), F32),
             pltpu.VMEM((8, 128, 1024), F32),
             pltpu.VMEM((1024, 1024), BF),

time: 86.5 us -> 78 us (0.902)
  Pallas kernels: 85.7 us -> 77.3 us
    pallas_call x1, Pallas kernels: 84 us -> 75.5 us  [per_device(): pl.pallas_call(kernel, out_shape=(pltpu.VMEM((128, 512), BF), pltpu.VMEM(...]
where the time goes in v3:
time: 78 us; the launch traced here: 77.9 us
  Pallas kernels  77.3 us (99%)
    pallas_call x1, Pallas kernels, per_device(): pl.pallas_call(kernel, out_shape=(pltpu.VMEM((128, 512), BF), pltpu.VMEM(...  75.5 us
    pallas_call x1, Pallas kernels, per_device(): pl.pallas_call(leave, out_shape=tuple((jax.ShapeDtypeStruct(o.shape, BF)...  1.74 us

profile of v3, /device:TPU:1, one launch (start us, length us, event | category | flops | bytes accessed | tf_op | source)
XLA Modules:
  0.0 77.9 jit_solution(98406708306471905)
XLA Ops:
  0.6 75.5 %shard_map.102 = (bf16[128,512]{1,0:T(8,128)(2,1)S(1)}, bf16[512,1024]{1,0:T(8,128)(2,1)S(1)}, bf16[512,1024]{1,0:T(8,128)(2,1)S(1)}, bf16[1024,512]{1,0:T(8,128)(2,1)S(1)}) custom-call(bf16[128,512]{1,0:T(8,128)(2,1)} %acts.1, bf16[128,512]{1,0:T(8,128)(2,1)} %grad.1, bf16[32,1024]{1,0:T(8,128)(2,1)} %gate.1, bf16[32,1024]{1,0:T(8,128)(2,1)} %up.1, ...), custom_call_target="tpu_custom_call" | custom-call | tf_op jit(solution)/shard_map/pallas_call | solution.py:517
  76.2 1.7 %shard_map.103 = (bf16[128,512]{1,0:T(8,128)(2,1)}, bf16[512,1024]{1,0:T(8,128)(2,1)}, bf16[512,1024]{1,0:T(8,128)(2,1)}, bf16[1024,512]{1,0:T(8,128)(2,1)}) custom-call(bf16[128,512]{1,0:T(8,128)(2,1)S(1)} %get-tuple-element.8.refs_0_, bf16[512,1024]{1,0:T(8,128)(2,1)S(1)} %get-tuple-element.9.refs_1_, bf16[512,1024]{1,0:T(8,128)(2,1)S(1)} %get-tuple-element.10.refs_2_, ...), custom_call_target="tpu_custom_call" | custom-call | tf_op jit(solution)/shard_map/pallas_call | solution.py:565

commit v4 on v3

--- a/solution.py
+++ b/solution.py
@@ -1,3 +1,5 @@
+import math
+
 import jax
 import jax.numpy as jnp
 from jax import lax
@@ -11,7 +13,9 @@
 NZ, NX = 8, 4
 CH = 2
 W = 1024 // CH
-N_SEM = 192
+N_RECV = 149
+N_SEND = 6
+UNIT = 32 * 1024
 
 
 def dot_nt(left, right):
@@ -73,11 +77,16 @@
     pl.semaphore_wait(barrier, 9)
 
     copies = {}
+    sent = [0]
 
     def send(name, src, dst, peer):
         i = len(copies)
+        units = math.prod(src.shape) * src.dtype.itemsize // UNIT
+        if sent[-1] + units > 64:
+            sent.append(0)
+        sent[-1] += units
         copy = pltpu.make_async_remote_copy(
-            src_ref=src, dst_ref=dst, send_sem=send_sem.at[i], recv_sem=recv_sem.at[i],
+            src_ref=src, dst_ref=dst, send_sem=send_sem.at[len(sent) - 1], recv_sem=recv_sem.at[i],
             device_id=peer, device_id_type=MESH,
         )
         copy.start()
@@ -499,8 +508,9 @@
         val = total(side, second, 1)
         got("yh%d" % side)
         o_in[:, 256 * side : 256 * side + 256] = (val + yr[side].astype(F32)).astype(BF)
-    for copy in copies.values():
-        copy.wait_send()
+    for i, units in enumerate(sent):
+        behind = hid.at[0 : 16 * units]
+        pltpu.make_async_copy(behind, behind, send_sem.at[i]).wait()
 
 
 def leave(*refs):
@@ -554,9 +564,9 @@
             pltpu.VMEM((2, 2, 128, 256), F32),
             pltpu.VMEM((2, 128, 256), BF),
             pltpu.VMEM((2, 128, 256), BF),
-            pltpu.SemaphoreType.DMA((N_SEM,)),
-            pltpu.SemaphoreType.DMA((N_SEM,)),
-            pltpu.SemaphoreType.DMA((12,)),
+            pltpu.SemaphoreType.DMA((N_SEND,)),
+            pltpu.SemaphoreType.DMA((N_RECV,)),
+            pltpu.SemaphoreType.DMA((7,)),
         ],
         compiler_params=pltpu.CompilerParams(
             collective_id=0, has_side_effects=True, vmem_limit_bytes=56 * 1024 * 1024

time: 78 us -> 75.7 us (0.971)
  Pallas kernels: 77.3 us -> 74.9 us
    pallas_call x1, Pallas kernels: 75.5 us -> 73.2 us  [per_device(): pl.pallas_call(kernel, out_shape=(pltpu.VMEM((128, 512), BF), pltpu.VMEM(...]
where the time goes in v4:
time: 75.7 us; the launch traced here: 75.6 us
  Pallas kernels  74.9 us (99%)
    pallas_call x1, Pallas kernels, per_device(): pl.pallas_call(kernel, out_shape=(pltpu.VMEM((128, 512), BF), pltpu.VMEM(...  73.2 us
    pallas_call x1, Pallas kernels, per_device(): pl.pallas_call(leave, out_shape=tuple((jax.ShapeDtypeStruct(o.shape, BF)...  1.74 us

profile of v4, /device:TPU:1, one launch (start us, length us, event | category | flops | bytes accessed | tf_op | source)
XLA Modules:
  0.0 75.6 jit_solution(5294469819778086984)
XLA Ops:
  0.6 73.2 %shard_map.102 = (bf16[128,512]{1,0:T(8,128)(2,1)S(1)}, bf16[512,1024]{1,0:T(8,128)(2,1)S(1)}, bf16[512,1024]{1,0:T(8,128)(2,1)S(1)}, bf16[1024,512]{1,0:T(8,128)(2,1)S(1)}) custom-call(bf16[128,512]{1,0:T(8,128)(2,1)} %acts.1, bf16[128,512]{1,0:T(8,128)(2,1)} %grad.1, bf16[32,1024]{1,0:T(8,128)(2,1)} %gate.1, bf16[32,1024]{1,0:T(8,128)(2,1)} %up.1, ...), custom_call_target="tpu_custom_call" | custom-call | tf_op jit(solution)/shard_map/pallas_call | solution.py:527
  73.8 1.7 %shard_map.103 = (bf16[128,512]{1,0:T(8,128)(2,1)}, bf16[512,1024]{1,0:T(8,128)(2,1)}, bf16[512,1024]{1,0:T(8,128)(2,1)}, bf16[1024,512]{1,0:T(8,128)(2,1)}) custom-call(bf16[128,512]{1,0:T(8,128)(2,1)S(1)} %get-tuple-element.8.refs_0_, bf16[512,1024]{1,0:T(8,128)(2,1)S(1)} %get-tuple-element.9.refs_1_, bf16[512,1024]{1,0:T(8,128)(2,1)S(1)} %get-tuple-element.10.refs_2_, ...), custom_call_target="tpu_custom_call" | custom-call | tf_op jit(solution)/shard_map/pallas_call | solution.py:575
